TPU v7x, 128 devices: a whole 4x4x4 slice. The times are simulated.
128 devices in a mesh: row: 8 (over x, core), col: 16 (over z, y).
Axes of the slice: x: 4, y: 4, z: 4, core: 2. Of those that a mesh axis runs over, the one named last changes fastest.
Arguments:
- features: bfloat16 [32768, 256], P('row'), may hold values from -6 to 6
- join_weight: bfloat16 [256, 256], replicated, may hold values from -0.375 to 0.375
- partner: int32 [32768], replicated, may hold values from 0 to 32767, as said below
- tile_index: int32 [13312], P(('row', 'col')), may hold values from 0 to 127, as said below
- tile_values: bfloat16 [13312, 256, 256], P(('row', 'col')), may hold values from 0 to 10
- pert_slot: int32 [512], P(('row', 'col')), may hold values from 0 to 103
- pert_values: bfloat16 [512, 256, 256], P(('row', 'col')), may hold values from 0 to 0.5
- routes: int32 [13312, 2], P(('row', 'col')), may hold values from 0 to 127, as said below
Outputs:
- coarse_features: bfloat16 [16384, 256], P('row')
- coarse_quarters: bfloat16 [32768, 128, 128], P(('row', 'col'))
Inputs may be any that keep to these rules, and one draw needn't show every extreme that they name: `partner`: fine nodes 16384 + k * 256 + j and k * 256 + s are partners of each other, where s runs over a permutation of the 256 slots for each coarse tile k. `tile_index`: each entry is a local tile position i * 8 + j with i below 16; the entries of one device are distinct; the four devices whose row indices agree modulo 8 // 2 and whose col indices agree modulo 16 // 2 hold the same list in the same order. `routes`: every column of a row equals column 0. Among the 104 rows of one device no device number appears more than 2 times, and in every draw some device number appears exactly 2 times among one device's rows.
All inputs are finite; a program needn't handle non-finite values.
Results may differ from a plain program's by a relative error of at most 0.0052.
Values may be sent and summed in bfloat16 or wider, within the bound.
No kernel may reach another device: no remote copies, remote signals or barrier semaphores. Data moves between devices by JAX's collectives and lax.ppermute only.
A program may use at most 192 MiB of HBM per device.

v0:
```python
import jax
import jax.numpy as jnp
from jax import lax
from jax.sharding import PartitionSpec as P


def swapped(value, axis, stride):
    mask = 2**stride
    pairs = [(source, source ^ mask) for source in range(lax.axis_size(axis))]
    return lax.ppermute(value, axis, pairs)


def pairing_table(slot_table, table_width):
    levels = lax.broadcasted_iota(jnp.int32, slot_table.shape + (table_width,), slot_table.ndim)
    return (slot_table[..., None] == levels).astype(jnp.bfloat16)


def keep_block(tile_block):
    return tile_block


def local(features, join_weight, partner, tile_index, tile_values, pert_slot, pert_values, routes):
    row_count = lax.axis_size("row")
    col_count = lax.axis_size("col")
    row_half = row_count // 2
    col_half = col_count // 2
    row_bit = row_count.bit_length() - 2
    col_bit = col_count.bit_length() - 2
    row_index = lax.axis_index("row")
    col_index = lax.axis_index("col")
    row_side = row_index // row_half
    col_side = col_index // col_half
    tile_size = tile_values.shape[1]
    half_tile = tile_size // 2
    slot_count = tile_values.shape[0]
    feat_width = features.shape[1]
    tiles_row = features.shape[0] // tile_size
    node_count = partner.shape[0]
    tiles_col = node_count // tile_size // col_count
    coarse_count = node_count // tile_size // 2
    coarse_nodes = coarse_count * tile_size
    capacity = routes.shape[1]
    receive_slots = row_count * col_count * capacity
    row_start = row_index % row_half * tiles_row
    col_start = col_index % col_half * tiles_col
    local_row = tile_index // tiles_col
    local_col = tile_index % tiles_col
    odd_slots = (
        partner[coarse_nodes:].reshape(coarse_count, tile_size)
        - (jnp.arange(coarse_count, dtype=jnp.int32) * tile_size)[:, None]
    )
    row_table = lax.dynamic_slice_in_dim(odd_slots, row_start, tiles_row, 0)
    col_table = lax.dynamic_slice_in_dim(odd_slots, col_start, tiles_col, 0)
    feature_tiles = features.reshape(tiles_row, tile_size, feat_width)

    def permute_features(tile_block):
        pair_table = pairing_table(row_table, tile_size)
        return jnp.einsum(
            "ijs,ijf->isf", pair_table, tile_block, preferred_element_type=jnp.float32
        ).astype(jnp.bfloat16)

    own_features = lax.cond(row_side == 1, permute_features, keep_block, feature_tiles)
    given_rows = lax.dynamic_slice_in_dim(own_features, (1 - row_side) * half_tile, half_tile, 1)
    kept_rows = lax.dynamic_slice_in_dim(own_features, row_side * half_tile, half_tile, 1)
    partner_features = swapped(given_rows, "row", row_bit)
    merged = (kept_rows.astype(jnp.float32) + partner_features.astype(jnp.float32)).astype(
        jnp.bfloat16
    )
    joined_rows = jnp.dot(
        merged.reshape(tiles_row * half_tile, feat_width),
        join_weight,
        preferred_element_type=jnp.float32,
    )
    extra_table = (pert_slot[:, None] == jnp.arange(slot_count, dtype=jnp.int32)[None, :]).astype(
        jnp.bfloat16
    )
    added_tiles = jnp.einsum(
        "pn,pxy->nxy", extra_table, pert_values, preferred_element_type=jnp.float32
    )
    perturbed = (tile_values.astype(jnp.float32) + added_tiles).astype(jnp.bfloat16)

    def permute_rows(tile_block):
        pair_table = pairing_table(row_table[local_row], tile_size)
        return jnp.einsum(
            "njs,njc->nsc", pair_table, tile_block, preferred_element_type=jnp.float32
        ).astype(jnp.bfloat16)

    def permute_cols(tile_block):
        pair_table = pairing_table(col_table[local_col], tile_size)
        return jnp.einsum(
            "nrj,njs->nrs", tile_block, pair_table, preferred_element_type=jnp.float32
        ).astype(jnp.bfloat16)

    paired = lax.cond(row_side == 1, permute_rows, keep_block, perturbed)
    paired = lax.cond(col_side == 1, permute_cols, keep_block, paired)
    row_given = lax.dynamic_slice_in_dim(paired, (1 - row_side) * half_tile, half_tile, 1)
    row_kept = lax.dynamic_slice_in_dim(paired, row_side * half_tile, half_tile, 1)
    row_partner = swapped(row_given, "row", row_bit)
    row_summed = row_kept.astype(jnp.float32) + row_partner.astype(jnp.float32)
    col_given = lax.dynamic_slice_in_dim(row_summed, (1 - col_side) * half_tile, half_tile, 2)
    col_kept = lax.dynamic_slice_in_dim(row_summed, col_side * half_tile, half_tile, 2)
    col_partner = swapped(col_given, "col", col_bit)
    quarter = col_kept + col_partner
    row_select = (local_row[None, :] == jnp.arange(tiles_row, dtype=jnp.int32)[:, None]).astype(
        jnp.float32
    )
    owned_sums = jnp.dot(
        row_select,
        jnp.sum(quarter, axis=2),
        precision=lax.Precision.HIGHEST,
        preferred_element_type=jnp.float32,
    )
    spread = jnp.zeros((2, row_half, tiles_row, half_tile), jnp.float32)
    spread = lax.dynamic_update_slice(
        spread, owned_sums[None, None], (row_side, row_index % row_half, 0, 0)
    )
    layout = lax.psum(spread, ("row", "col"))
    degree = (
        1.0 + jnp.transpose(layout, (1, 2, 0, 3)).reshape(coarse_count, tile_size) / coarse_nodes
    )
    row_degree = lax.dynamic_slice(
        degree, (row_start, row_side * half_tile), (tiles_row, half_tile)
    )
    col_degree = lax.dynamic_slice(
        degree, (col_start, col_side * half_tile), (tiles_col, half_tile)
    )
    slot_row_degree = row_degree[local_row]
    slot_col_degree = col_degree[local_col]
    normalized = (
        quarter / jnp.sqrt(slot_row_degree[:, :, None] * slot_col_degree[:, None, :])
    ).astype(jnp.bfloat16)
    coarse_features = (
        joined_rows.reshape(tiles_row, half_tile, feat_width) / jnp.sqrt(row_degree)[:, :, None]
    ).astype(jnp.bfloat16)
    coarse_features = coarse_features.reshape(tiles_row * half_tile, feat_width)
    targets = routes[:, 0]
    slot_order = jnp.arange(slot_count, dtype=jnp.int32)
    earlier = jnp.sum(
        (
            (targets[:, None] == targets[None, :]) & (slot_order[None, :] < slot_order[:, None])
        ).astype(jnp.int32),
        axis=1,
    )
    position = targets * capacity + earlier
    place_table = (position[None, :] == jnp.arange(receive_slots, dtype=jnp.int32)[:, None]).astype(
        jnp.bfloat16
    )
    outgoing = jnp.dot(
        place_table,
        normalized.reshape(slot_count, half_tile * half_tile),
        preferred_element_type=jnp.float32,
    ).astype(jnp.bfloat16)
    arrived = lax.all_to_all(
        outgoing.reshape(receive_slots, half_tile, half_tile),
        ("row", "col"),
        split_axis=0,
        concat_axis=0,
        tiled=True,
    )
    return (coarse_features, arrived)


def solution(mesh):
    placed = (
        P("row", None),
        P(),
        P(),
        P(("row", "col")),
        P(("row", "col"), None, None),
        P(("row", "col")),
        P(("row", "col"), None, None),
        P(("row", "col"), None),
    )
    return jax.shard_map(
        local,
        mesh=mesh,
        in_specs=placed,
        out_specs=(P("row", None), P(("row", "col"), None, None)),
        check_vma=False,
    )
```

profile of v0, /device:TPU:32, one launch (start us, length us, event | category | flops | bytes accessed | tf_op | source)
XLA Modules:
  0.0 729.7 jit_solution(8674809250563732469)
XLA Ops:
  7.3 0.9 slice.16
  8.9 17.9 %add_convert_fusion = bf16[104,256,256]{2,0,1:T(8,128)(2,1)} fusion(bf16[104,256,256]{2,1,0:T(8,128)(2,1)} %param.18, bf16[4,256,256]{2,1,0:T(8,128)(2,1)S(1)} %copy-done, s32[4]{0:T(128)} %param.19), kind=kOutput, calls=%fused_computation.22 | convolution fusion | flops 74973600 | bytes 27787280 | tf_op jit(solution)/shard_map/pn,pxy->nxy/dot_general | solution.py:77
  26.9 10.9 %conditional.4 = (bf16[104,256,256]{2,1,0:T(8,128)(2,1)}) conditional(s32[]{:T(128)} %convert_element_type.62, (bf16[104,256,256]{2,0,1:T(8,128)(2,1)}) %tuple.35, (s32[104]{0:T(128)S(1)}, s32[16,256]{1,0:T(8,128)S(1)}, bf16[104,256,256]{2,0,1:T(8,128)(2,1)}) %tuple.29), branch_computations={%region_2.3_spmd, %region_3.4_spmd} | conditional | flops 3503293696 | bytes 27588232 | solution.py:94
  26.9 10.9 %copy.30 = bf16[104,256,256]{2,1,0:T(8,128)(2,1)} copy(bf16[104,256,256]{2,0,1:T(8,128)(2,1)} %get-tuple-element.61) | data formatting | bytes 27262976 | tf_op jit(solution)/shard_map/convert_element_type | solution.py:80
  37.8 18.4 %conditional.5 = (bf16[104,256,256]{1,2,0:T(8,128)(2,1)}) conditional(s32[]{:T(128)} %convert_element_type.66, (bf16[104,256,256]{2,1,0:T(8,128)(2,1)}) %conditional.4, (s32[64,256]{1,0:T(8,128)S(1)}, s32[]{:T(128)}, s32[104]{0:T(128)S(1)}, bf16[104,256,256]{2,1,0:T(8,128)(2,1)}) %tuple.30), branch_computations={%region_4.5_spmd, %region_5.6_spmd} | conditional | flops 3503293696 | bytes 27604620 | solution.py:95
  37.8 18.4 %copy.31 = bf16[104,256,256]{1,2,0:T(8,128)(2,1)} copy(bf16[104,256,256]{2,1,0:T(8,128)(2,1)} %get-tuple-element.63) | data formatting | bytes 27262976 | tf_op jit(solution)/shard_map/cond | solution.py:94
  56.2 6.7 constant_dynamic-slice_fusion.2
  62.9 11.1 %collective-permute-start.1 = (bf16[104,128,256]{1,2,0:T(8,128)(2,1)}, bf16[104,128,256]{1,2,0:T(8,128)(2,1)}, u32[]{:S(2)}, u32[]{:S(2)}) collective-permute-start(bf16[104,128,256]{1,2,0:T(8,128)(2,1)} %constant_dynamic-slice_fusion.2), channel_id=1, source_target_pairs={{0,64},{16,80},{32,96},{48,112},{64,0},{80,16},{96,32},{112,48},{1... | collective-permute-start | bytes 20447240 | tf_op jit(solution)/shard_map/ppermute | solution.py:10
  73.9 147.1 %collective-permute-done.1 = bf16[104,128,256]{1,2,0:T(8,128)(2,1)} collective-permute-done((bf16[104,128,256]{1,2,0:T(8,128)(2,1)}, bf16[104,128,256]{1,2,0:T(8,128)(2,1)}, u32[]{:S(2)}, u32[]{:S(2)}) %collective-permute-start.1) | collective-permute-done | bytes 6815776 | tf_op jit(solution)/shard_map/ppermute | solution.py:10
  221.0 12.7 %convert_add_fusion = f32[104,128,256]{1,2,0:T(8,128)} fusion(bf16[104,128,256]{1,2,0:T(8,128)(2,1)} %collective-permute-done.1, bf16[104,256,256]{1,2,0:T(8,128)(2,1)} %get-tuple-element.80, s32[]{:T(128)S(6)} %select_n.77), kind=kLoop, calls=%fused_computation.24 | loop fusion | flops 10223616 | bytes 27262980 | tf_op jit(solution)/shard_map/add | solution.py:99
  233.7 6.7 constant_dynamic-slice_fusion.1
  240.4 8.8 %collective-permute-start.2 = (f32[104,128,128]{1,2,0:T(8,128)}, f32[104,128,128]{1,2,0:T(8,128)}, u32[]{:S(2)}, u32[]{:S(2)}) collective-permute-start(f32[104,128,128]{1,2,0:T(8,128)} %constant_dynamic-slice_fusion.1), channel_id=1, source_target_pairs={{0,8},{1,9},{2,10},{3,11},{4,12},{5,13},{6,14},{7,15},{8,0},{9,1},... | collective-permute-start | bytes 20447240 | tf_op jit(solution)/shard_map/ppermute | solution.py:10
  249.4 146.3 %collective-permute-done.2 = f32[104,128,128]{1,2,0:T(8,128)} collective-permute-done((f32[104,128,128]{1,2,0:T(8,128)}, f32[104,128,128]{1,2,0:T(8,128)}, u32[]{:S(2)}, u32[]{:S(2)}) %collective-permute-start.2) | collective-permute-done | bytes 6815776 | tf_op jit(solution)/shard_map/ppermute | solution.py:10
  395.7 6.7 fusion.14
  403.2 140.7 %all-reduce.2.cloned.1.call-done = f32[2,4,16,128]{3,2,1,0:T(8,128)} async-done(((f32[2,4,16,128]{3,2,1,0:T(8,128)}), f32[2,4,16,128]{3,2,1,0:T(8,128)}) %all-reduce.2.cloned.1.call-update) | async-done | bytes 65552 | tf_op jit(solution)/shard_map/psum | solution.py:117
  546.1 8.4 %multiply_convert_fusion = bf16[104,128,128]{1,2,0:T(8,128)(2,1)} fusion(f32[104,128]{1,0:T(8,128)S(1)} %gather_fusion.3, f32[104,128]{1,0:T(8,128)S(1)} %gather_fusion.2, f32[104,128,128]{1,2,0:T(8,128)} %collective-permute-done.2, f32[104,128,256]{1,2,0:T(8,128)} %convert_add_fusion, s32[]{:T(128)S(6)} %select_n.84), kind=kLoop, calls=%fused_computation.25 | loop fusion | flops 6815744 | bytes 17145860 | tf_op jit(solution)/shard_map/convert_element_type | solution.py:131
  554.5 5.8 copy.29
  560.3 8.3 %fusion.11 = bf16[32,8,128,128]{3,1,2,0:T(8,128)(2,1)} fusion(bf16[13,8,128,128]{3,2,1,0:T(8,128)(2,1)} %bitcast.36, s32[104]{0:T(128)S(1)} %multiply_add_fusion), kind=kOutput, calls=%fused_computation.27 | convolution fusion | flops 876636160 | bytes 11796896 | tf_op jit(solution)/shard_map/dot_general | solution.py:148
  568.7 9.2 %copy.34 = bf16[32,8,128,128]{3,2,1,0:T(8,128)(2,1)} copy(bf16[32,8,128,128]{3,1,2,0:T(8,128)(2,1)} %fusion.11) | data formatting | bytes 16777216
  577.9 6.9 all-to-all-start
  584.9 4.1 collective-permute-start
  589.0 121.7 %collective-permute-done = bf16[16,128,256]{2,1,0:T(8,128)(2,1)S(1)} collective-permute-done((bf16[16,128,256]{2,1,0:T(8,128)(2,1)S(1)}, bf16[16,128,256]{2,1,0:T(8,128)(2,1)S(1)}, u32[]{:S(2)}, u32[]{:S(2)}) %collective-permute-start) | collective-permute-done | bytes 1048608 | tf_op jit(solution)/shard_map/ppermute | solution.py:10
  710.7 1.5 divide_convert_fusion
  712.2 10.6 %copy.61 = bf16[256,128,128]{2,1,0:T(8,128)(2,1)} copy(bf16[256,128,128]{2,1,0:T(8,128)(2,1)} %all-to-all-done) | data formatting | bytes 16777216
  (35 shorter events, 4.1 us)
Async XLA Ops:
  7.2 1.7 copy-start
  7.2 536.8 %all-reduce.2.cloned.1.call-start = ((), (), s32[]{:S(2)}) async-start(), calls=%async_computation.1 | async-start | bytes 131072 | tf_op jit(solution)/shard_map/psum | solution.py:117
  62.9 158.1 %collective-permute-start.1 = (bf16[104,128,256]{1,2,0:T(8,128)(2,1)}, bf16[104,128,256]{1,2,0:T(8,128)(2,1)}, u32[]{:S(2)}, u32[]{:S(2)}) collective-permute-start(bf16[104,128,256]{1,2,0:T(8,128)(2,1)} %constant_dynamic-slice_fusion.2), channel_id=1, source_target_pairs={{0,64},{16,80},{32,96},{48,112},{64,0},{80,16},{96,32},{112,48},{1... | collective-permute-start | bytes 20447240 | tf_op jit(solution)/shard_map/ppermute | solution.py:10
  233.7 15.5 %copy-start.5 = (s32[104,2]{0,1:T(2,128)S(1)}, s32[104,2]{0,1:T(2,128)}, u32[]{:S(2)}) copy-start(s32[104,2]{0,1:T(2,128)} %param.21) | copy-start | bytes 2500
  240.4 155.3 %collective-permute-start.2 = (f32[104,128,128]{1,2,0:T(8,128)}, f32[104,128,128]{1,2,0:T(8,128)}, u32[]{:S(2)}, u32[]{:S(2)}) collective-permute-start(f32[104,128,128]{1,2,0:T(8,128)} %constant_dynamic-slice_fusion.1), channel_id=1, source_target_pairs={{0,8},{1,9},{2,10},{3,11},{4,12},{5,13},{6,14},{7,15},{8,0},{9,1},... | collective-permute-start | bytes 20447240 | tf_op jit(solution)/shard_map/ppermute | solution.py:10
  402.5 0.6 copy-start.3
  577.9 6.9 copy-start.2
  577.9 134.3 %all-to-all-start = ((bf16[256,128,128]{2,1,0:T(8,128)(2,1)}), bf16[256,128,128]{2,1,0:T(8,128)(2,1)}, u32[]{:S(2)}, u32[]{:S(2)}) async-start(bf16[256,128,128]{2,1,0:T(8,128)(2,1)} %bitcast.35), calls=%async_computation | async-start | bytes 16777216 | tf_op jit(solution)/shard_map/all_to_all | solution.py:153
  584.8 125.9 %copy-start.4 = (bf16[256,256]{1,0:T(8,128)(2,1)S(1)}, bf16[256,256]{1,0:T(8,128)(2,1)}, u32[]{:S(2)}) copy-start(bf16[256,256]{1,0:T(8,128)(2,1)} %param.15) | copy-start | bytes 393220
  584.9 125.8 %collective-permute-start = (bf16[16,128,256]{2,1,0:T(8,128)(2,1)S(1)}, bf16[16,128,256]{2,1,0:T(8,128)(2,1)S(1)}, u32[]{:S(2)}, u32[]{:S(2)}) collective-permute-start(bf16[16,128,256]{2,1,0:T(8,128)(2,1)S(1)} %constant_dynamic-slice_fusion.3), channel_id=1, source_target_pairs={{0,64},{16,80},{32,96},{48,112},{64,0},{80,16},{96,32},{112,48},{1... | collective-permute-start | bytes 3145736 | tf_op jit(solution)/shard_map/ppermute | solution.py:10
  712.2 10.6 %copy-start.1 = (bf16[4,256,256]{2,1,0:T(8,128)(2,1)S(1)}, bf16[4,256,256]{2,1,0:T(8,128)(2,1)}, u32[]{:S(2)}) copy-start(bf16[4,256,256]{2,1,0:T(8,128)(2,1)} %param.20) | copy-start | bytes 1572868
Sparse Core Ops, SparseCore 0:
  403.3 140.5 all-reduce.1
where the time goes:
time: 731 us; the launch traced here: 730 us
  waiting for transfers between devices  556 us (76%)
  local copies, waits for them, and re-layouts  71.3 us (10%)
  starting transfers between devices  30.9 us (4%)
  other arithmetic  29.6 us (4%)
  matrix products  27.9 us (4%)
  between operations  14.2 us (2%)
    ppermute x3, waiting for transfers between devices, swapped(): return lax.ppermute(value, axis, pairs)  415 us
    psum x1, waiting for transfers between devices, local(): layout = lax.psum(spread, ('row', 'col'))  141 us
    ppermute x3, starting transfers between devices, swapped(): return lax.ppermute(value, axis, pairs)  23.9 us
    unnamed x15, local copies, waits for them, and re-layouts  20.5 us
    cond x1, local copies, waits for them, and re-layouts, local(): paired = lax.cond(row_side == 1, permute_rows, keep_block, perturbed)  18.4 us
    dot_general x1, matrix products, local(): jnp.einsum('pn,pxy->nxy', extra_table, pert_values, preferred_element_typ...  17.9 us
  transfers between devices with their start and end apart: 5, of which 4 were waited for; matrix products, arithmetic and copies ran while one was open for 0% of the time, Pallas kernels for 0%

commit v1 on v0

--- a/solution.py
+++ b/solution.py
@@ -114,7 +114,8 @@
     spread = lax.dynamic_update_slice(
         spread, owned_sums[None, None], (row_side, row_index % row_half, 0, 0)
     )
-    layout = lax.psum(spread, ("row", "col"))
+    terms = lax.all_gather(spread, ("row", "col"))
+    layout = jnp.sum(terms, axis=0)
     degree = (
         1.0 + jnp.transpose(layout, (1, 2, 0, 3)).reshape(coarse_count, tile_size) / coarse_nodes
     )

time: 731 us -> 664 us (0.908)
  waiting for transfers between devices: 556 us -> 485 us
    psum x1 -> x0, waiting for transfers between devices: 141 us -> none  [local(): layout = lax.psum(spread, ('row', 'col'))]
    all_gather x0 -> x1, waiting for transfers between devices: none -> 70.4 us  [local(): terms = lax.all_gather(spread, ('row', 'col'))]
where the time goes in v1:
time: 664 us; the launch traced here: 663 us
  waiting for transfers between devices  485 us (73%)
  local copies, waits for them, and re-layouts  71.3 us (11%)
  other arithmetic  32.6 us (5%)
  starting transfers between devices  31.9 us (5%)
  matrix products  27.9 us (4%)
  between operations  14.2 us (2%)
    ppermute x3, waiting for transfers between devices, swapped(): return lax.ppermute(value, axis, pairs)  415 us
    all_gather x1, waiting for transfers between devices, local(): terms = lax.all_gather(spread, ('row', 'col'))  70.4 us
    ppermute x3, starting transfers between devices, swapped(): return lax.ppermute(value, axis, pairs)  24.2 us
    unnamed x15, local copies, waits for them, and re-layouts  20.5 us
    cond x1, local copies, waits for them, and re-layouts, local(): paired = lax.cond(row_side == 1, permute_rows, keep_block, perturbed)  18.4 us
    dot_general x1, matrix products, local(): jnp.einsum('pn,pxy->nxy', extra_table, pert_values, preferred_element_typ...  17.9 us
  transfers between devices with their start and end apart: 5, of which 4 were waited for; matrix products, arithmetic and copies ran while one was open for 0% of the time, Pallas kernels for 0%

profile of v1, /device:TPU:32, one launch (start us, length us, event | category | flops | bytes accessed | tf_op | source)
XLA Modules:
  0.0 663.3 jit_solution(11039430712430083147)
XLA Ops:
  8.9 17.9 %add_convert_fusion = bf16[104,256,256]{2,0,1:T(8,128)(2,1)} fusion(bf16[104,256,256]{2,1,0:T(8,128)(2,1)} %param.18, bf16[4,256,256]{2,1,0:T(8,128)(2,1)S(1)} %copy-done, s32[4]{0:T(128)} %param.19), kind=kOutput, calls=%fused_computation.22 | convolution fusion | flops 74973600 | bytes 27787280 | tf_op jit(solution)/shard_map/pn,pxy->nxy/dot_general | solution.py:77
  26.9 10.9 %conditional.4 = (bf16[104,256,256]{2,1,0:T(8,128)(2,1)}) conditional(s32[]{:T(128)} %convert_element_type.62, (bf16[104,256,256]{2,0,1:T(8,128)(2,1)}) %tuple.36, (s32[104]{0:T(128)S(1)}, s32[16,256]{1,0:T(8,128)S(1)}, bf16[104,256,256]{2,0,1:T(8,128)(2,1)}) %tuple.29), branch_computations={%region_2.3_spmd, %region_3.4_spmd} | conditional | flops 3503293696 | bytes 27588232 | solution.py:94
  26.9 10.9 %copy.35 = bf16[104,256,256]{2,1,0:T(8,128)(2,1)} copy(bf16[104,256,256]{2,0,1:T(8,128)(2,1)} %get-tuple-element.64) | data formatting | bytes 27262976 | tf_op jit(solution)/shard_map/convert_element_type | solution.py:80
  37.8 18.4 %conditional.5 = (bf16[104,256,256]{1,2,0:T(8,128)(2,1)}) conditional(s32[]{:T(128)} %convert_element_type.66, (bf16[104,256,256]{2,1,0:T(8,128)(2,1)}) %conditional.4, (s32[64,256]{1,0:T(8,128)S(1)}, s32[]{:T(128)}, s32[104]{0:T(128)S(1)}, bf16[104,256,256]{2,1,0:T(8,128)(2,1)}) %tuple.30), branch_computations={%region_4.5_spmd, %region_5.6_spmd} | conditional | flops 3503293696 | bytes 27604620 | solution.py:95
  37.8 18.4 %copy.36 = bf16[104,256,256]{1,2,0:T(8,128)(2,1)} copy(bf16[104,256,256]{2,1,0:T(8,128)(2,1)} %get-tuple-element.66) | data formatting | bytes 27262976 | tf_op jit(solution)/shard_map/cond | solution.py:94
  56.2 6.7 %constant_dynamic-slice_fusion.2 = bf16[104,128,256]{1,2,0:T(8,128)(2,1)} fusion(bf16[104,256,256]{1,2,0:T(8,128)(2,1)} %get-tuple-element.83, s32[]{:T(128)S(6)} %select_n.78), kind=kLoop, calls=%fused_computation.54 | loop fusion | bytes 13631492 | tf_op jit(solution)/shard_map/dynamic_slice | solution.py:96
  62.9 11.1 %collective-permute-start.1 = (bf16[104,128,256]{1,2,0:T(8,128)(2,1)}, bf16[104,128,256]{1,2,0:T(8,128)(2,1)}, u32[]{:S(2)}, u32[]{:S(2)}) collective-permute-start(bf16[104,128,256]{1,2,0:T(8,128)(2,1)} %constant_dynamic-slice_fusion.2), channel_id=1, source_target_pairs={{0,64},{16,80},{32,96},{48,112},{64,0},{80,16},{96,32},{112,48},{1... | collective-permute-start | bytes 20447240 | tf_op jit(solution)/shard_map/ppermute | solution.py:10
  73.9 147.1 %collective-permute-done.1 = bf16[104,128,256]{1,2,0:T(8,128)(2,1)} collective-permute-done((bf16[104,128,256]{1,2,0:T(8,128)(2,1)}, bf16[104,128,256]{1,2,0:T(8,128)(2,1)}, u32[]{:S(2)}, u32[]{:S(2)}) %collective-permute-start.1) | collective-permute-done | bytes 6815776 | tf_op jit(solution)/shard_map/ppermute | solution.py:10
  221.0 12.7 %convert_add_fusion = f32[104,128,256]{1,2,0:T(8,128)} fusion(bf16[104,128,256]{1,2,0:T(8,128)(2,1)} %collective-permute-done.1, bf16[104,256,256]{1,2,0:T(8,128)(2,1)} %get-tuple-element.83, s32[]{:T(128)S(6)} %select_n.77), kind=kLoop, calls=%fused_computation.24 | loop fusion | flops 10223616 | bytes 27262980 | tf_op jit(solution)/shard_map/add | solution.py:99
  233.7 6.7 %constant_dynamic-slice_fusion.1 = f32[104,128,128]{1,2,0:T(8,128)} fusion(f32[104,128,256]{1,2,0:T(8,128)} %convert_add_fusion, s32[]{:T(128)S(6)} %select_n.85), kind=kLoop, calls=%fused_computation.53 | loop fusion | bytes 13631492 | tf_op jit(solution)/shard_map/dynamic_slice | solution.py:100
  240.4 8.8 %collective-permute-start.2 = (f32[104,128,128]{1,2,0:T(8,128)}, f32[104,128,128]{1,2,0:T(8,128)}, u32[]{:S(2)}, u32[]{:S(2)}) collective-permute-start(f32[104,128,128]{1,2,0:T(8,128)} %constant_dynamic-slice_fusion.1), channel_id=1, source_target_pairs={{0,8},{1,9},{2,10},{3,11},{4,12},{5,13},{6,14},{7,15},{8,0},{9,1},... | collective-permute-start | bytes 20447240 | tf_op jit(solution)/shard_map/ppermute | solution.py:10
  249.2 146.5 %collective-permute-done.2 = f32[104,128,128]{1,2,0:T(8,128)} collective-permute-done((f32[104,128,128]{1,2,0:T(8,128)}, f32[104,128,128]{1,2,0:T(8,128)}, u32[]{:S(2)}, u32[]{:S(2)}) %collective-permute-start.2) | collective-permute-done | bytes 6815776 | tf_op jit(solution)/shard_map/ppermute | solution.py:10
  395.7 6.7 %fusion.14 = f32[104,128]{1,0:T(8,128)S(1)} fusion(f32[104,128,128]{1,2,0:T(8,128)} %collective-permute-done.2, f32[104,128,256]{1,2,0:T(8,128)} %convert_add_fusion, s32[]{:T(128)S(6)} %select_n.84), kind=kLoop, calls=%fused_computation.30 | loop fusion | flops 3394560 | bytes 13684740 | tf_op jit(solution)/shard_map/reduce_sum | solution.py:109
  403.4 70.4 %all-gather.2.cloned.1.call-done = f32[128,2,4,16,128]{4,3,2,1,0:T(8,128)} async-done(((f32[1,2,4,16,128]{4,3,2,1,0:T(8,128)}), f32[128,2,4,16,128]{4,3,2,1,0:T(8,128)}) %all-gather.2.cloned.1.call-update) | async-done | bytes 8388624 | tf_op jit(solution)/shard_map/all_gather | solution.py:117
  473.8 3.9 reduce_sum.28
  479.0 8.4 %multiply_convert_fusion = bf16[104,128,128]{1,2,0:T(8,128)(2,1)} fusion(f32[104,128]{1,0:T(8,128)S(1)} %gather_fusion.3, f32[104,128]{1,0:T(8,128)S(1)} %gather_fusion.2, f32[104,128,128]{1,2,0:T(8,128)} %collective-permute-done.2, f32[104,128,256]{1,2,0:T(8,128)} %convert_add_fusion, s32[]{:T(128)S(6)} %select_n.84), kind=kLoop, calls=%fused_computation.25 | loop fusion | flops 6815744 | bytes 17145860 | tf_op jit(solution)/shard_map/convert_element_type | solution.py:132
  487.4 5.8 copy.34
  493.2 8.3 %fusion.11 = bf16[32,8,128,128]{3,1,2,0:T(8,128)(2,1)} fusion(bf16[13,8,128,128]{3,2,1,0:T(8,128)(2,1)} %bitcast.36, s32[104]{0:T(128)S(1)} %multiply_add_fusion), kind=kOutput, calls=%fused_computation.27 | convolution fusion | flops 876636160 | bytes 11796896 | tf_op jit(solution)/shard_map/dot_general | solution.py:149
  501.6 9.2 %copy.39 = bf16[32,8,128,128]{3,2,1,0:T(8,128)(2,1)} copy(bf16[32,8,128,128]{3,1,2,0:T(8,128)(2,1)} %fusion.11) | data formatting | bytes 16777216
  510.8 7.7 %all-to-all-start = ((bf16[256,128,128]{2,1,0:T(8,128)(2,1)}), bf16[256,128,128]{2,1,0:T(8,128)(2,1)}, u32[]{:S(2)}, u32[]{:S(2)}) async-start(bf16[256,128,128]{2,1,0:T(8,128)(2,1)} %bitcast.35), calls=%async_computation | async-start | bytes 16777216 | tf_op jit(solution)/shard_map/all_to_all | solution.py:154
  518.6 4.3 collective-permute-start
  522.9 121.5 %collective-permute-done = bf16[16,128,256]{2,1,0:T(8,128)(2,1)S(1)} collective-permute-done((bf16[16,128,256]{2,1,0:T(8,128)(2,1)S(1)}, bf16[16,128,256]{2,1,0:T(8,128)(2,1)S(1)}, u32[]{:S(2)}, u32[]{:S(2)}) %collective-permute-start) | collective-permute-done | bytes 1048608 | tf_op jit(solution)/shard_map/ppermute | solution.py:10
  644.4 1.5 divide_convert_fusion
  645.8 10.6 %copy.65 = bf16[256,128,128]{2,1,0:T(8,128)(2,1)} copy(bf16[256,128,128]{2,1,0:T(8,128)(2,1)} %all-to-all-done) | data formatting | bytes 16777216
  (36 shorter events, 4.2 us)
Async XLA Ops:
  7.2 1.7 copy-start
  7.2 466.6 %all-gather.2.cloned.1.call-start = ((), (), s32[]{:S(2)}) async-start(), calls=%async_computation.1 | async-start | bytes 8454144 | tf_op jit(solution)/shard_map/all_gather | solution.py:117
  62.9 158.1 %collective-permute-start.1 = (bf16[104,128,256]{1,2,0:T(8,128)(2,1)}, bf16[104,128,256]{1,2,0:T(8,128)(2,1)}, u32[]{:S(2)}, u32[]{:S(2)}) collective-permute-start(bf16[104,128,256]{1,2,0:T(8,128)(2,1)} %constant_dynamic-slice_fusion.2), channel_id=1, source_target_pairs={{0,64},{16,80},{32,96},{48,112},{64,0},{80,16},{96,32},{112,48},{1... | collective-permute-start | bytes 20447240 | tf_op jit(solution)/shard_map/ppermute | solution.py:10
  240.4 155.3 %collective-permute-start.2 = (f32[104,128,128]{1,2,0:T(8,128)}, f32[104,128,128]{1,2,0:T(8,128)}, u32[]{:S(2)}, u32[]{:S(2)}) collective-permute-start(f32[104,128,128]{1,2,0:T(8,128)} %constant_dynamic-slice_fusion.1), channel_id=1, source_target_pairs={{0,8},{1,9},{2,10},{3,11},{4,12},{5,13},{6,14},{7,15},{8,0},{9,1},... | collective-permute-start | bytes 20447240 | tf_op jit(solution)/shard_map/ppermute | solution.py:10
  249.2 154.0 %copy-start.5 = (s32[104,2]{0,1:T(2,128)S(1)}, s32[104,2]{0,1:T(2,128)}, u32[]{:S(2)}) copy-start(s32[104,2]{0,1:T(2,128)} %param.21) | copy-start | bytes 2500
  402.5 0.6 copy-start.3
  510.8 7.7 %copy-start.2 = (bf16[4096,256]{1,0:T(8,128)(2,1)S(1)}, bf16[4096,256]{1,0:T(8,128)(2,1)}, u32[]{:S(2)}) copy-start(bf16[4096,256]{1,0:T(8,128)(2,1)} %param.14) | copy-start | bytes 6291460
  510.8 135.1 %all-to-all-start = ((bf16[256,128,128]{2,1,0:T(8,128)(2,1)}), bf16[256,128,128]{2,1,0:T(8,128)(2,1)}, u32[]{:S(2)}, u32[]{:S(2)}) async-start(bf16[256,128,128]{2,1,0:T(8,128)(2,1)} %bitcast.35), calls=%async_computation | async-start | bytes 16777216 | tf_op jit(solution)/shard_map/all_to_all | solution.py:154
  518.4 125.9 %copy-start.4 = (bf16[256,256]{1,0:T(8,128)(2,1)S(1)}, bf16[256,256]{1,0:T(8,128)(2,1)}, u32[]{:S(2)}) copy-start(bf16[256,256]{1,0:T(8,128)(2,1)} %param.15) | copy-start | bytes 393220
  518.6 125.8 %collective-permute-start = (bf16[16,128,256]{2,1,0:T(8,128)(2,1)S(1)}, bf16[16,128,256]{2,1,0:T(8,128)(2,1)S(1)}, u32[]{:S(2)}, u32[]{:S(2)}) collective-permute-start(bf16[16,128,256]{2,1,0:T(8,128)(2,1)S(1)} %constant_dynamic-slice_fusion.3), channel_id=1, source_target_pairs={{0,64},{16,80},{32,96},{48,112},{64,0},{80,16},{96,32},{112,48},{1... | collective-permute-start | bytes 3145736 | tf_op jit(solution)/shard_map/ppermute | solution.py:10
  645.8 10.6 %copy-start.1 = (bf16[4,256,256]{2,1,0:T(8,128)(2,1)S(1)}, bf16[4,256,256]{2,1,0:T(8,128)(2,1)}, u32[]{:S(2)}) copy-start(bf16[4,256,256]{2,1,0:T(8,128)(2,1)} %param.20) | copy-start | bytes 1572868
Sparse Core Ops, SparseCore 0:
  403.3 70.4 all-gather.1
